TPU v7x, 512 devices: a whole 4x4x16 slice. The times are simulated.
512 devices in a mesh: tok: 32 (over y, x, core), voc: 16 (over z).
Axes of the slice: x: 4, y: 4, z: 16, core: 2. Of those that a mesh axis runs over, the one named last changes fastest.
Arguments:
- student_hidden: bfloat16 [512, 2560], P('tok', 'voc'), may hold values from -72 to 72
- teacher_rows: bfloat16 [512, 4096], P('tok', 'voc'), may hold values from -72 to 72
- student_head: bfloat16 [2560, 131072], P(None, ('tok', 'voc')), may hold values from -0.375 to 0.375
- teacher_head: bfloat16 [4096, 131072], P(None, ('tok', 'voc')), may hold values from -0.25 to 0.25
- lengths: int32 [32], replicated, may hold values from 1 to 16, 320 in all
- route: int32 [512], replicated, may hold values from 0 to 511, each once
- sampled_ids: int32 [512], replicated, may hold values from 0 to 131071
- mix_flags: int32 [512], replicated, may hold values 0 or 1
Outputs:
- divergence: float32 [512], P('tok')
- head_grad: bfloat16 [2560, 131072], P(None, ('tok', 'voc'))
Inputs may be any that keep to these rules, and one draw needn't show every extreme that they name: The lengths sum to 320; the largest is exactly 16. `route`: each trainer position appears once.
All inputs are finite; a program needn't handle non-finite values.
Results may differ from a plain program's by a relative error of at most 0.0052.
Values may be sent and summed in bfloat16 or wider, within the bound.
No kernel may reach another device: no remote copies, remote signals or barrier semaphores. Data moves between devices by JAX's collectives and lax.ppermute only.
A program may use at most 64 MiB of HBM per device.

v0:
```python
import jax
import jax.numpy as jnp
from jax import lax
from jax.sharding import PartitionSpec as P


def on_device(
    student_hidden, teacher_rows, student_head, teacher_head, lengths, route, sampled_ids, mix_flags
):
    tok_count = lax.axis_size("tok")
    voc_count = lax.axis_size("voc")
    group = lax.axis_index("tok")
    grp_rows = student_hidden.shape[0]
    vocab_dev = student_head.shape[1]
    first_col = (group * voc_count + lax.axis_index("voc")) * vocab_dev
    local_s, local_t = (student_hidden, teacher_rows)
    trainer_of = jnp.arange(grp_rows * tok_count, dtype=jnp.int32)
    live_rows = (trainer_of % grp_rows < lengths[trainer_of // grp_rows]).astype(jnp.float32)
    full_s, full_t = (
        lax.all_gather(local_s, "voc", axis=1, tiled=True),
        lax.all_gather(local_t, "voc", axis=1, tiled=True),
    )
    rows_s = lax.all_gather(full_s, "tok", axis=0, tiled=True)
    gathered = jnp.dot(
        lax.all_gather(full_t, "tok", axis=0, tiled=True),
        teacher_head,
        preferred_element_type=jnp.float32,
    )
    inverse = jnp.zeros_like(route).at[route].set(jnp.arange(route.shape[0], dtype=jnp.int32))
    teacher_logits = gathered[inverse]
    student_logits = jnp.dot(rows_s, student_head, preferred_element_type=jnp.float32)
    row_ids = sampled_ids[trainer_of]
    row_flags = mix_flags[trainer_of]
    onehot = row_ids[:, None] - first_col == jnp.arange(vocab_dev, dtype=jnp.int32)[None, :]
    pick_s = jnp.sum(jnp.where(onehot, student_logits, 0.0), axis=1)
    pick_u = jnp.sum(jnp.where(onehot, teacher_logits, 0.0), axis=1)
    s_max, u_max = lax.pmax(
        (jnp.max(student_logits, axis=1), jnp.max(teacher_logits, axis=1)), ("tok", "voc")
    )
    s_sum = jnp.sum(jnp.exp(student_logits - s_max[:, None]), axis=1)
    u_sum = jnp.sum(jnp.exp(teacher_logits - u_max[:, None]), axis=1)
    s_tot, u_tot, pick_s, pick_u = lax.psum((s_sum, u_sum, pick_s, pick_u), ("tok", "voc"))
    lse_s = s_max + jnp.log(s_tot)
    lse_u = u_max + jnp.log(u_tot)
    log_student = student_logits - lse_s[:, None]
    log_teacher = teacher_logits - lse_u[:, None]
    probs = jnp.exp(log_student)
    gap = log_student - log_teacher
    kl_all = lax.psum(jnp.sum(probs * gap, axis=1), ("tok", "voc"))
    mixed = 1.0 / (0.2 * jnp.exp(pick_u - lse_u - (pick_s - lse_s)) + 0.8)
    weight = jnp.where(row_flags == 1, mixed, jnp.ones_like(mixed))
    dlogits = ((live_rows * weight)[:, None] * probs * (gap - kl_all[:, None])).astype(jnp.bfloat16)
    head_grad = lax.dot_general(
        rows_s, dlogits, (((0,), (0,)), ((), ())), preferred_element_type=jnp.float32
    )
    kl_rows = live_rows * kl_all
    divergence = lax.dynamic_slice_in_dim(kl_rows, group * grp_rows, grp_rows)
    return (divergence, head_grad.astype(jnp.bfloat16))


def solution(mesh):
    in_specs = (
        P("tok", "voc"),
        P("tok", "voc"),
        P(None, ("tok", "voc")),
        P(None, ("tok", "voc")),
        P(),
        P(),
        P(),
        P(),
    )
    out_specs = (P("tok"), P(None, ("tok", "voc")))
    return jax.shard_map(
        on_device, mesh=mesh, in_specs=in_specs, out_specs=out_specs, check_vma=False
    )
```

profile of v0, /device:TPU:1, one launch (start us, length us, event | category | flops | bytes accessed | tf_op | source)
XLA Modules:
  0.0 505.5 jit_solution(3653330909238869689)
XLA Ops:
  7.3 30.2 %all-gather = bf16[16,160,16]{1,2,0:T(8,128)(2,1)S(1)} all-gather(bf16[1,160,16]{1,2,0:T(8,128)(2,1)} %bitcast.47), channel_id=1, replica_groups=mesh['tok'=32,'voc'=16] {'voc'}, dimensions={0}, use_global_device_ids=true | all-gather | bytes 87040 | tf_op jit(solution)/shard_map/all_gather | solution.py:20
  37.5 0.8 reshape.200
  38.4 22.4 %all_gather.14 = bf16[16,4096]{1,0:T(8,128)(2,1)} all-gather(bf16[16,256]{1,0:T(8,128)(2,1)} %param.9), channel_id=1, replica_groups=mesh['tok'=32,'voc'=16] {'voc'}, dimensions={1}, use_global_device_ids=true | all-gather | bytes 139264 | tf_op jit(solution)/shard_map/all_gather | solution.py:21
  60.8 3.6 gather_fusion.2
  64.4 3.5 gather_fusion.1
  68.0 2.4 scatter_custom_fusion
  71.3 0.7 fusion.14
  72.0 4.3 compare_select_fusion.1
  76.4 0.7 fusion.13
  77.1 24.5 %all-gather.4.cloned.1.call-done = bf16[512,2560]{1,0:T(8,128)(2,1)} async-done(((bf16[16,2560]{1,0:T(8,128)(2,1)}), bf16[512,2560]{1,0:T(8,128)(2,1)}) %all-gather.4.cloned.1.call-update) | async-done | bytes 2621456 | tf_op jit(solution)/shard_map/all_gather | solution.py:23
  101.6 3.8 fusion.15
  105.4 60.2 %all-gather.6.cloned.1.call-done = bf16[512,4096]{1,0:T(8,128)(2,1)} async-done(((bf16[16,4096]{1,0:T(8,128)(2,1)}), bf16[512,4096]{1,0:T(8,128)(2,1)}) %all-gather.6.cloned.1.call-update) | async-done | bytes 4194320 | tf_op jit(solution)/shard_map/all_gather | solution.py:25
  165.6 3.4 fusion.16
  169.1 1.6 gather_fusion
  170.7 1.0 copy.18
  171.8 103.7 %all-reduce.2 = (f32[512]{0:T(512)S(1)}, f32[512]{0:T(512)S(1)}) all-reduce(f32[512]{0:T(512)S(1)} %reduce_max.19, f32[512]{0:T(512)S(1)} %get-tuple-element.52), channel_id=1, replica_groups=mesh['tok'=32,'voc'=16] {'tok','voc'}, use_global_device_ids=true, to_apply=%region_6.7 | all-reduce | flops 1024 | bytes 8192 | tf_op jit(solution)/shard_map/pmax | solution.py:37
  275.7 1.2 exponential_reduce_fusion.1
  276.9 100.3 %all-reduce.1 = (f32[512]{0:T(512)S(1)}, f32[512]{0:T(512)S(1)}) all-reduce(f32[512]{0:T(512)S(1)} %exponential_reduce_fusion, f32[512]{0:T(512)S(1)} %exponential_reduce_fusion.1), channel_id=1, replica_groups=mesh['tok'=32,'voc'=16] {'tok','voc'}, use_global_device_ids=true, to_apply=%region_8.9 | all-reduce | flops 1024 | bytes 8192 | tf_op jit(solution)/shard_map/psum | solution.py:42
  377.2 1.3 select_reduce_fusion.1
  378.5 99.5 %all-reduce = (f32[512]{0:T(512)S(1)}, f32[512]{0:T(512)S(1)}, f32[512]{0:T(512)S(1)}) all-reduce(f32[512]{0:T(512)S(1)} %get-tuple-element.9, f32[512]{0:T(512)S(1)} %get-tuple-element.10, f32[512]{0:T(512)S(1)} %get-tuple-element.8), channel_id=1, replica_groups=mesh['tok'=32,'voc'=16] {'tok','voc'}, use_global_device_ids=true, to_apply=%region_10.11 | all-reduce | flops 1536 | bytes 12288 | tf_op jit(solution)/shard_map/psum | solution.py:49
  478.0 15.7 %fusion.5 = (f32[512]{0:T(512)S(1)}, pred[512]{0:T(512)(128)(4,1)S(1)}) fusion(f32[512]{0:T(512)S(1)} %get-tuple-element.12, f32[512]{0:T(512)S(1)} %get-tuple-element.55, f32[512]{0:T(512)S(1)} %get-tuple-element.13, f32[512]{0:T(512)S(1)} %get-tuple-element.54, s32[512]{0:T(512)S(1)} %gather_fusion.1, pred[512]{0:T(512)(128)(4,1)S(1)} %compare_reduce_fusion, ...), kind=kLoop, calls=%fused_computation.60 | loop fusion | flops 20992 | bytes 27748 | tf_op jit(solution)/shard_map/mul | solution.py:52
  493.7 2.9 fusion
  496.7 1.4 copy.20
  498.1 0.6 dynamic_slice.3
  (51 shorter events, 1.5 us)
Async XLA Ops:
  7.2 158.5 %copy-start = (bf16[4096,256]{1,0:T(8,128)(2,1)S(1)}, bf16[4096,256]{1,0:T(8,128)(2,1)}, u32[]{:S(2)}) copy-start(bf16[4096,256]{1,0:T(8,128)(2,1)} %param.11) | copy-start | bytes 6291460
  7.2 57.3 %copy-start.1 = (s32[512]{0:T(512)S(1)}, s32[512]{0:T(512)}, u32[]{:S(2)}) copy-start(s32[512]{0:T(512)} %param.15) | copy-start | bytes 6148
  7.2 60.8 %copy-start.4 = (s32[512]{0:T(512)S(1)}, s32[512]{0:T(512)}, u32[]{:S(2)}) copy-start(s32[512]{0:T(512)} %param.13) | copy-start | bytes 6148
  7.2 94.4 %all-gather.4.cloned.1.call-start = ((), (), s32[]{:S(2)}) async-start(), calls=%async_computation | async-start | bytes 2703360 | tf_op jit(solution)/shard_map/all_gather | solution.py:23
  7.2 64.0 %copy-start.3 = (s32[32]{0:T(128)S(1)}, s32[32]{0:T(128)}, u32[]{:S(2)}) copy-start(s32[32]{0:T(128)} %param.12) | copy-start | bytes 388
  38.4 127.3 %all-gather.6.cloned.1.call-start = ((), (), s32[]{:S(2)}) async-start(), calls=%async_computation.1 | async-start | bytes 4325376 | tf_op jit(solution)/shard_map/all_gather | solution.py:25
  170.7 206.5 %copy-start.2 = (f32[512,256]{0,1:T(8,128)S(1)}, f32[512,256]{0,1:T(8,128)}, u32[]{:S(2)}) copy-start(f32[512,256]{0,1:T(8,128)} %get-tuple-element.53) | copy-start | bytes 1572868
Sparse Core Ops, SparseCore 0:
  38.5 63.0 all-gather.3
  104.7 60.8 all-gather.5
where the time goes:
time: 506 us
  blocking collectives  356 us (70%)
  waiting for transfers between devices  84.7 us (17%)
  other arithmetic  23.8 us (5%)
  local copies, waits for them, and re-layouts  16.5 us (3%)
  between operations  14.2 us (3%)
  matrix products  10.2 us (2%)
    pmax x1, blocking collectives, on_device(): lax.pmax((jnp.max(student_logits, axis=1), jnp.max(teacher_logits, axis=1...  104 us
    psum x1, blocking collectives, on_device(): lax.psum((s_sum, u_sum, pick_s, pick_u), ('tok', 'voc'))  100 us
    psum x1, blocking collectives, on_device(): kl_all = lax.psum(jnp.sum(probs * gap, axis=1), ('tok', 'voc'))  99.5 us
    all_gather x1, waiting for transfers between devices, on_device(): lax.all_gather(full_t, 'tok', axis=0, tiled=True)  60.2 us
    all_gather x1, blocking collectives, on_device(): lax.all_gather(local_s, 'voc', axis=1, tiled=True)  30.2 us
    all_gather x1, waiting for transfers between devices, on_device(): rows_s = lax.all_gather(full_s, 'tok', axis=0, tiled=True)  24.5 us
    all_gather x1, blocking collectives, on_device(): lax.all_gather(local_t, 'voc', axis=1, tiled=True)  22.4 us
    mul x1, other arithmetic, on_device(): live_rows * weight  15.7 us
  transfers between devices with their start and end apart: 2, of which 2 were waited for; matrix products, arithmetic and copies ran while one was open for 4% of the time, Pallas kernels for 0%

commit v1 on v0

--- a/solution.py
+++ b/solution.py
@@ -22,7 +22,9 @@
     )
     rows_s = lax.all_gather(full_s, "tok", axis=0, tiled=True)
     gathered = jnp.dot(
-        lax.all_gather(full_t, "tok", axis=0, tiled=True),
+        jnp.concatenate(
+            lax.all_to_all(jnp.stack([full_t] * lax.axis_size("tok")), "tok", 0, 0), axis=0
+        ),
         teacher_head,
         preferred_element_type=jnp.float32,
     )

time: 506 us -> 479 us (0.947)
  waiting for transfers between devices: 84.7 us -> 38.7 us
  starting transfers between devices: 0.08 us -> 22 us
    all_gather x1 -> x0, waiting for transfers between devices: 60.2 us -> none  [on_device(): lax.all_gather(full_t, 'tok', axis=0, tiled=True)]
    all_to_all x0 -> x1, waiting for transfers between devices: none -> 38.6 us  [on_device(): lax.all_to_all(jnp.stack([full_t] * lax.axis_size('tok')), 'tok', 0, 0)]
    all_gather x1, waiting for transfers between devices: 24.5 us -> 0.02 us  [on_device(): rows_s = lax.all_gather(full_s, 'tok', axis=0, tiled=True)]
    all_to_all x0 -> x1, starting transfers between devices: none -> 22 us  [on_device(): lax.all_to_all(jnp.stack([full_t] * lax.axis_size('tok')), 'tok', 0, 0)]
  transfers between devices with their start and end apart: 2 -> 2, of which waited for: 2 -> 1; matrix products, arithmetic and copies ran while one was open for 4% -> 5% of each run, Pallas kernels for 0% -> 0%
where the time goes in v1:
time: 479 us; the launch traced here: 478 us
  blocking collectives  352 us (73%)
  waiting for transfers between devices  38.7 us (8%)
  other arithmetic  23.6 us (5%)
  starting transfers between devices  22 us (5%)
  local copies, waits for them, and re-layouts  18 us (4%)
  between operations  14.3 us (3%)
  matrix products  10.2 us (2%)
    pmax x1, blocking collectives, on_device(): lax.pmax((jnp.max(student_logits, axis=1), jnp.max(teacher_logits, axis=1...  102 us
    psum x1, blocking collectives, on_device(): kl_all = lax.psum(jnp.sum(probs * gap, axis=1), ('tok', 'voc'))  100 us
    psum x1, blocking collectives, on_device(): lax.psum((s_sum, u_sum, pick_s, pick_u), ('tok', 'voc'))  99.5 us
    all_to_all x1, waiting for transfers between devices, on_device(): lax.all_to_all(jnp.stack([full_t] * lax.axis_size('tok')), 'tok', 0, 0)  38.6 us
    all_gather x1, blocking collectives, on_device(): lax.all_gather(local_s, 'voc', axis=1, tiled=True)  30.2 us
    all_to_all x1, starting transfers between devices, on_device(): lax.all_to_all(jnp.stack([full_t] * lax.axis_size('tok')), 'tok', 0, 0)  22 us
    all_gather x1, blocking collectives, on_device(): lax.all_gather(local_t, 'voc', axis=1, tiled=True)  20 us
    mul x1, other arithmetic, on_device(): live_rows * weight  15.6 us
  transfers between devices with their start and end apart: 2, of which 1 were waited for; matrix products, arithmetic and copies ran while one was open for 5% of the time, Pallas kernels for 0%

profile of v1, /device:TPU:1, one launch (start us, length us, event | category | flops | bytes accessed | tf_op | source)
XLA Modules:
  0.0 478.3 jit_solution(2305605284519569021)
XLA Ops:
  7.2 30.2 %all-gather = bf16[16,160,16]{1,2,0:T(8,128)(2,1)S(1)} all-gather(bf16[1,160,16]{1,2,0:T(8,128)(2,1)} %bitcast.48), channel_id=1, replica_groups=mesh['tok'=32,'voc'=16] {'voc'}, dimensions={0}, use_global_device_ids=true | all-gather | bytes 87040 | tf_op jit(solution)/shard_map/all_gather | solution.py:20
  37.5 0.8 reshape.206
  38.3 20.0 %all_gather.11 = bf16[16,4096]{1,0:T(8,128)(2,1)S(1)} all-gather(bf16[16,256]{1,0:T(8,128)(2,1)} %param.9), channel_id=1, replica_groups=mesh['tok'=32,'voc'=16] {'voc'}, dimensions={1}, use_global_device_ids=true | all-gather | bytes 139264 | tf_op jit(solution)/shard_map/all_gather | solution.py:21
  58.3 2.5 stack.2
  60.8 22.0 %all-to-all-start = ((bf16[32,16,4096]{2,1,0:T(8,128)(2,1)}), bf16[32,16,4096]{2,1,0:T(8,128)(2,1)}, u32[]{:S(2)}, u32[]{:S(2)}) async-start(bf16[32,16,4096]{2,1,0:T(8,128)(2,1)} %stack.2), calls=%async_computation | async-start | bytes 8388608 | tf_op jit(solution)/shard_map/all_to_all | solution.py:26
  82.8 3.5 gather_fusion.2
  86.3 3.5 gather_fusion.1
  89.9 2.4 scatter_custom_fusion
  93.2 0.7 fusion.14
  93.9 4.3 compare_select_fusion.1
  98.2 0.7 fusion.13
  99.0 38.6 %all-to-all-done = bf16[32,16,4096]{2,1,0:T(8,128)(2,1)} async-done(((bf16[32,16,4096]{2,1,0:T(8,128)(2,1)}), bf16[32,16,4096]{2,1,0:T(8,128)(2,1)}, u32[]{:S(2)}, u32[]{:S(2)}) %all-to-all-start) | async-done | bytes 4194336 | tf_op jit(solution)/shard_map/all_to_all | solution.py:26
  137.6 3.4 fusion.16
  141.1 1.6 gather_fusion
  143.0 3.8 fusion.15
  146.8 101.7 %all-reduce.2 = (f32[512]{0:T(512)S(1)}, f32[512]{0:T(512)S(1)}) all-reduce(f32[512]{0:T(512)S(1)} %reduce_max.19, f32[512]{0:T(512)S(1)} %get-tuple-element.52), channel_id=1, replica_groups=mesh['tok'=32,'voc'=16] {'tok','voc'}, use_global_device_ids=true, to_apply=%region_6.7 | all-reduce | flops 1024 | bytes 8192 | tf_op jit(solution)/shard_map/pmax | solution.py:39
  248.8 1.2 exponential_reduce_fusion.1
  250.0 99.5 %all-reduce.1 = (f32[512]{0:T(512)S(1)}, f32[512]{0:T(512)S(1)}) all-reduce(f32[512]{0:T(512)S(1)} %exponential_reduce_fusion, f32[512]{0:T(512)S(1)} %exponential_reduce_fusion.1), channel_id=1, replica_groups=mesh['tok'=32,'voc'=16] {'tok','voc'}, use_global_device_ids=true, to_apply=%region_8.9 | all-reduce | flops 1024 | bytes 8192 | tf_op jit(solution)/shard_map/psum | solution.py:44
  349.5 1.3 select_reduce_fusion.1
  350.8 100.1 %all-reduce = (f32[512]{0:T(512)S(1)}, f32[512]{0:T(512)S(1)}, f32[512]{0:T(512)S(1)}) all-reduce(f32[512]{0:T(512)S(1)} %get-tuple-element.9, f32[512]{0:T(512)S(1)} %get-tuple-element.10, f32[512]{0:T(512)S(1)} %get-tuple-element.8), channel_id=1, replica_groups=mesh['tok'=32,'voc'=16] {'tok','voc'}, use_global_device_ids=true, to_apply=%region_10.11 | all-reduce | flops 1536 | bytes 12288 | tf_op jit(solution)/shard_map/psum | solution.py:51
  450.9 15.6 %fusion.5 = (f32[512]{0:T(512)S(1)}, pred[512]{0:T(512)(128)(4,1)S(1)}) fusion(f32[512]{0:T(512)S(1)} %get-tuple-element.12, f32[512]{0:T(512)S(1)} %get-tuple-element.55, f32[512]{0:T(512)S(1)} %get-tuple-element.13, f32[512]{0:T(512)S(1)} %get-tuple-element.54, s32[512]{0:T(512)S(1)} %gather_fusion.1, pred[512]{0:T(512)(128)(4,1)S(1)} %compare_reduce_fusion, ...), kind=kLoop, calls=%fused_computation.60 | loop fusion | flops 20992 | bytes 27748 | tf_op jit(solution)/shard_map/mul | solution.py:54
  466.5 2.9 fusion
  469.5 1.4 copy.20
  470.9 0.6 dynamic_slice.3
  (53 shorter events, 1.6 us)
Async XLA Ops:
  7.2 130.5 %copy-start = (bf16[4096,256]{1,0:T(8,128)(2,1)S(1)}, bf16[4096,256]{1,0:T(8,128)(2,1)}, u32[]{:S(2)}) copy-start(bf16[4096,256]{1,0:T(8,128)(2,1)} %param.11) | copy-start | bytes 6291460
  7.2 135.9 %all-gather.3.cloned.1.call-start = ((), (), s32[]{:S(2)}) async-start(), calls=%async_computation.1 | async-start | bytes 2703360 | tf_op jit(solution)/shard_map/all_gather | solution.py:23
  60.8 22.1 %copy-start.1 = (s32[512]{0:T(512)S(1)}, s32[512]{0:T(512)}, u32[]{:S(2)}) copy-start(s32[512]{0:T(512)} %param.14) | copy-start | bytes 6148
  60.8 76.9 %all-to-all-start = ((bf16[32,16,4096]{2,1,0:T(8,128)(2,1)}), bf16[32,16,4096]{2,1,0:T(8,128)(2,1)}, u32[]{:S(2)}, u32[]{:S(2)}) async-start(bf16[32,16,4096]{2,1,0:T(8,128)(2,1)} %stack.2), calls=%async_computation | async-start | bytes 8388608 | tf_op jit(solution)/shard_map/all_to_all | solution.py:26
  82.8 3.6 copy-start.2
  82.8 7.1 %copy-start.5 = (s32[512]{0:T(512)S(1)}, s32[512]{0:T(512)}, u32[]{:S(2)}) copy-start(s32[512]{0:T(512)} %param.13) | copy-start | bytes 6148
  82.8 10.4 %copy-start.4 = (s32[32]{0:T(128)S(1)}, s32[32]{0:T(128)}, u32[]{:S(2)}) copy-start(s32[32]{0:T(128)} %param.12) | copy-start | bytes 388
  142.9 206.7 %copy-start.3 = (f32[512,256]{0,1:T(8,128)}, f32[512,256]{0,1:T(8,128)S(1)}, u32[]{:S(2)}) copy-start(f32[512,256]{0,1:T(8,128)S(1)} %copy.18) | copy-start | bytes 1572868
Sparse Core Ops, SparseCore 0:
  38.4 97.1 all-gather.2
